TPU v7x, 512 devices: a whole 4x8x8 slice. The times are simulated.
512 devices in a mesh: subj: 8 (over z), vox: 64 (over y, x, core).
Axes of the slice: x: 4, y: 8, z: 8, core: 2. Of those that a mesh axis runs over, the one named last changes fastest.
Arguments:
- data: bfloat16 [8, 450, 65536], P('subj', None, 'vox'), may hold values from -6 to 6
- maps: bfloat16 [8, 256, 65536], P('subj', None, 'vox'), may hold values from -0.0234375 to 0.0234375
Outputs:
- response: float32 [450, 256], replicated
- new_maps: bfloat16 [8, 256, 65536], P('subj', None, 'vox')
All inputs are finite; a program needn't handle non-finite values.
Results may differ from a plain program's by a relative error of at most 0.0043.
The roundings to bfloat16 on the way count: a program that leaves them out, or rounds other values in their place, can miss the bound.
Values sent between devices are 32-bit elements; how exact they have to be, the bound alone decides.
A program may use at most 64 MiB of HBM per device.

v0:
```python
import jax
import jax.numpy as jnp
from jax import lax
from jax.sharding import Mesh
from jax.sharding import PartitionSpec as P

NS_STEPS = 5
VOX = ("vox_0", "vox_1", "vox_2")


def cut_along(shard, dim, size):
    before, after = (shard.shape[:dim], shard.shape[dim + 1 :])
    return jnp.moveaxis(shard.reshape(*before, size, -1, *after), dim, 0)


def sum_at_owner(shard, axis, dim):
    parts = cut_along(shard, dim, lax.axis_size(axis))
    arrived = lax.all_to_all(parts, axis, split_axis=0, concat_axis=0, tiled=True)
    return arrived.sum(axis=0)


def sum_by_axis(shard, axes, dim):
    far, near = axes
    parts = cut_along(shard, dim, lax.axis_size(far))
    nearer = sum_at_owner(parts, near, dim + 1)
    arrived = lax.all_to_all(nearer, far, split_axis=0, concat_axis=0, tiled=True)
    return arrived.sum(axis=0)


def from_everyone(shard, axis):
    size = lax.axis_size(axis)
    return lax.all_to_all(
        jnp.broadcast_to(shard[None], (size, *shard.shape)), axis, 0, 0, tiled=True
    )


def over_copies(shard, axis):
    everything = from_everyone(shard, axis)
    return jnp.sum(everything, axis=0)


def laid_out(parts, dim):
    parts = jnp.moveaxis(parts, 0, dim)
    dims = parts.shape
    return parts.reshape(*dims[:dim], dims[dim] * dims[dim + 1], *dims[dim + 2 :])


def gathered_copies(shard, axis, dim):
    return laid_out(from_everyone(shard, axis), dim)


def filled_up(lines, size):
    spare = -len(lines) % size
    return jnp.pad(lines, [(0, spare)] + [(0, 0)] * (lines.ndim - 1))


def gather_axes(shard, axes, dim):
    far, near = axes
    first = from_everyone(shard, far)
    parts = jnp.swapaxes(from_everyone(first, near), 0, 1)
    return laid_out(parts.reshape(-1, *shard.shape), dim)


def total_of(shard, axes):
    lines = shard.reshape(-1, shard.shape[-1])
    padded = filled_up(lines, lax.axis_size(axes[0]) * lax.axis_size(axes[1]))
    whole = gather_axes(sum_by_axis(padded, axes, 0), axes, 0)
    return lax.slice_in_dim(whole, 0, len(lines)).reshape(shard.shape)


def whiten(gram):
    scale = jnp.sqrt(jnp.sum(gram * gram, axis=(1, 2)) + 1e-06)[:, None, None]
    present_estimate = gram / scale
    eye = jnp.broadcast_to(jnp.eye(gram.shape[1], dtype=jnp.float32), gram.shape)
    inverse = eye
    for step in range(NS_STEPS):
        middle = 1.5 * eye - 0.5 * jnp.einsum(
            "sij,sjk->sik", inverse, present_estimate, precision=lax.Precision.HIGHEST
        )
        present_estimate = jnp.einsum(
            "sij,sjk->sik", present_estimate, middle, precision=lax.Precision.HIGHEST
        )
        inverse = jnp.einsum("sij,sjk->sik", middle, inverse, precision=lax.Precision.HIGHEST)
    return inverse / jnp.sqrt(scale)


def shards(data, maps):
    participant_count = lax.axis_size("subj") * data.shape[0]
    present_estimate = maps
    running_partial = jnp.einsum(
        "gqf,gmf->qm", data, present_estimate, preferred_element_type=jnp.float32
    )
    share = sum_by_axis(running_partial, (("vox_0", "vox_1"), "vox_2"), 1)
    share = over_copies(share, "subj")
    total = gathered_copies(share, VOX, 1)
    response = total / participant_count
    common_signal = response.astype(jnp.bfloat16)
    projected_signal = jnp.einsum(
        "go,zgj->zoj", common_signal, data, preferred_element_type=jnp.float32
    )
    local_gram = jnp.einsum(
        "dtc,drc->dtr", projected_signal, projected_signal, precision=lax.Precision.HIGHEST
    )
    gram = total_of(local_gram, (("vox_0", "vox_1"), "vox_2"))
    subject_factor = whiten(gram)
    present_estimate = jnp.einsum(
        "czm,cmj->czj", subject_factor, projected_signal, precision=lax.Precision.HIGHEST
    ).astype(jnp.bfloat16)
    return (response, present_estimate)


def solution(mesh):
    split = Mesh(
        mesh.devices.reshape(mesh.shape["subj"], 8, 4, 2), ("subj", "vox_0", "vox_1", "vox_2")
    )
    return jax.shard_map(
        shards,
        mesh=split,
        in_specs=(P("subj", None, VOX), P("subj", None, VOX)),
        out_specs=(P(), P("subj", None, VOX)),
        check_vma=False,
    )
```

profile of v0, /device:TPU:1, one launch (start us, length us, event | category | flops | bytes accessed | tf_op | source)
XLA Modules:
  0.0 122.8 jit_solution(10504816153789843135)
XLA Ops:
  0.6 0.0 copy-start
  0.6 1.2 copy-done
  1.8 1.6 %fusion.8 = f32[450,32,8]{0,1,2:T(8,128)S(1)} fusion(bf16[1,450,1024]{2,1,0:T(8,128)(2,1)S(1)} %copy-done, bf16[32,8,1024]{2,1,0:T(8,128)(2,1)} %bitcast.61), kind=kOutput, calls=%fused_computation.16 | convolution fusion | flops 235929600 | bytes 1906688 | tf_op jit(solution)/shard_map/gqf,gmf->qm/dot_general | solution.py:90
  3.4 10.6 %all_to_all.40 = f32[2,32,450,4]{2,1,3,0:T(8,128)S(1)} all-to-all(f32[2,32,450,4]{2,1,3,0:T(8,128)S(1)} %bitcast.60), channel_id=1, replica_groups=mesh['subj'=8,'vox_0'=8,'vox_1'=4,'vox_2'=2] {'vox_2'}, dimensions={0} | all-to-all | bytes 921600 | tf_op jit(solution)/shard_map/all_to_all | solution.py:18
  14.1 0.2 copy.15
  14.3 15.7 %all_to_all.41 = f32[32,450,4]{1,2,0:T(4,128)S(1)} all-to-all(f32[32,450,4]{1,2,0:T(4,128)S(1)} %copy.15), channel_id=1, replica_groups=mesh['subj'=8,'vox_0'=8,'vox_1'=4,'vox_2'=2] {'vox_0','vox_1'}, dimensions={0} | all-to-all | bytes 460800 | tf_op jit(solution)/shard_map/all_to_all | solution.py:26
  30.0 0.1 reduce_sum.55
  30.1 17.1 %all_to_all.42 = f32[8,450,4]{1,2,0:T(4,128)S(1)} all-to-all(f32[8,450,4]{1,2,0:T(4,128)S(1)} %broadcast_in_dim.8), channel_id=1, replica_groups=mesh['subj'=8,'vox_0'=8,'vox_1'=4,'vox_2'=2] {'subj'}, dimensions={0} | all-to-all | bytes 115200 | tf_op jit(solution)/shard_map/all_to_all | solution.py:32
  47.2 0.1 broadcast_in_dim.9
  47.2 25.2 %all_to_all.43 = f32[64,450,4]{1,2,0:T(4,128)S(1)} all-to-all(f32[64,450,4]{1,2,0:T(4,128)S(1)} %broadcast_in_dim.9), channel_id=1, replica_groups=mesh['subj'=8,'vox_0'=8,'vox_1'=4,'vox_2'=2] {'vox_0','vox_1','vox_2'}, dimensions={0} | all-to-all | bytes 921600 | tf_op jit(solution)/shard_map/all_to_all | solution.py:32
  72.5 0.2 fusion.13
  72.6 0.1 convert_element_type.18
  72.8 0.4 fusion.10
  73.2 0.3 dot_general.61
  73.5 1.6 %convolution_bitcast_fusion = f32[2,32,4,256]{3,1,2,0:T(8,128)S(1)} fusion(f32[256,1024]{1,0:T(8,128)S(1)} %fusion.10, f32[32,2,4,1024]{3,2,1,0:T(4,128)S(1)} %dot_general.61), kind=kOutput, calls=%fused_computation.13 | convolution fusion | flops 805306368 | bytes 2359296 | tf_op jit(solution)/shard_map/dtc,drc->dtr/dot_general | solution.py:101
  75.1 4.0 %all_to_all.44 = f32[2,32,4,256]{3,1,2,0:T(8,128)S(1)} all-to-all(f32[2,32,4,256]{3,1,2,0:T(8,128)S(1)} %convolution_bitcast_fusion), channel_id=1, replica_groups=mesh['subj'=8,'vox_0'=8,'vox_1'=4,'vox_2'=2] {'vox_2'}, dimensions={0} | all-to-all | bytes 524288 | tf_op jit(solution)/shard_map/all_to_all | solution.py:18
  79.1 0.1 copy.17
  79.2 14.0 %all_to_all.45 = f32[32,4,256]{2,1,0:T(4,128)S(1)} all-to-all(f32[32,4,256]{2,1,0:T(4,128)S(1)} %copy.17), channel_id=1, replica_groups=mesh['subj'=8,'vox_0'=8,'vox_1'=4,'vox_2'=2] {'vox_0','vox_1'}, dimensions={0} | all-to-all | bytes 262144 | tf_op jit(solution)/shard_map/all_to_all | solution.py:26
  93.2 0.7 broadcast_in_dim.10
  93.9 3.9 %all-to-all-start.6 = ((f32[32,4,256]{2,1,0:T(4,128)}), f32[32,4,256]{2,1,0:T(4,128)S(1)}, u32[]{:S(2)}, u32[]{:S(2)}) async-start(f32[32,4,256]{2,1,0:T(4,128)} %broadcast_in_dim.10), calls=%async_computation.6 | async-start | bytes 262144 | tf_op jit(solution)/shard_map/all_to_all | solution.py:32
  97.8 0.2 div.42
  98.0 1.0 copy.19
  98.9 8.2 %all-to-all-done.6 = f32[32,4,256]{2,1,0:T(4,128)S(1)} async-done(((f32[32,4,256]{2,1,0:T(4,128)}), f32[32,4,256]{2,1,0:T(4,128)S(1)}, u32[]{:S(2)}, u32[]{:S(2)}) %all-to-all-start.6) | async-done | bytes 131104 | tf_op jit(solution)/shard_map/all_to_all | solution.py:32
  107.2 7.0 %all_to_all.46 = f32[2,32,4,256]{3,2,1,0:T(4,128)S(1)} all-to-all(f32[2,32,4,256]{3,2,1,0:T(4,128)S(1)} %broadcast_in_dim.11), channel_id=1, replica_groups=mesh['subj'=8,'vox_0'=8,'vox_1'=4,'vox_2'=2] {'vox_2'}, dimensions={0} | all-to-all | bytes 524288 | tf_op jit(solution)/shard_map/all_to_all | solution.py:32
  114.1 0.7 multiply_reduce_fusion
  115.7 0.1 div.46
  115.8 0.3 fusion.5
  116.1 0.4 fusion.15
  116.5 0.3 fusion.14
  116.8 0.4 fusion.4
  117.1 0.4 fusion.17
  117.5 0.4 fusion.16
  117.9 0.4 fusion.3
  118.3 0.4 fusion.19
  118.7 0.4 fusion.18
  119.1 0.4 fusion.2
  119.5 0.4 fusion.20
  119.9 0.4 fusion.21
  120.2 0.4 fusion.1
  120.6 0.4 convolution_divide_fusion
  121.0 1.8 %fusion = bf16[1,256,1024]{2,1,0:T(8,128)(2,1)} fusion(f32[256,256]{1,0:T(8,128)S(1)} %convolution_divide_fusion, f32[256,1024]{1,0:T(8,128)S(1)} %fusion.10), kind=kOutput, calls=%fused_computation.1 | convolution fusion | flops 805568512 | bytes 1835008 | tf_op jit(solution)/shard_map/czm,cmj->czj/dot_general | solution.py:106
  (8 shorter events, 0.2 us)
Async XLA Ops:
  0.6 1.2 copy-start
  93.9 13.2 %all-to-all-start.6 = ((f32[32,4,256]{2,1,0:T(4,128)}), f32[32,4,256]{2,1,0:T(4,128)S(1)}, u32[]{:S(2)}, u32[]{:S(2)}) async-start(f32[32,4,256]{2,1,0:T(4,128)} %broadcast_in_dim.10), calls=%async_computation.6 | async-start | bytes 262144 | tf_op jit(solution)/shard_map/all_to_all | solution.py:32
where the time goes:
time: 123 us
  blocking collectives  93.5 us (76%)
  matrix products  10.6 us (9%)
  waiting for transfers between devices  8.2 us (7%)
  local copies, waits for them, and re-layouts  3.92 us (3%)
  starting transfers between devices  3.88 us (3%)
  between operations  1.6 us (1%)
    all_to_all x3, blocking collectives, from_everyone(): lax.all_to_all(jnp.broadcast_to(shard[None], (size, *shard.shape)), axis,...  49.2 us
    all_to_all x2, blocking collectives, sum_by_axis(): lax.all_to_all(nearer, far, split_axis=0, concat_axis=0, tiled=True)  29.7 us
    all_to_all x2, blocking collectives, sum_at_owner(): lax.all_to_all(parts, axis, split_axis=0, concat_axis=0, tiled=True)  14.6 us
    all_to_all x1, waiting for transfers between devices, from_everyone(): lax.all_to_all(jnp.broadcast_to(shard[None], (size, *shard.shape)), axis,...  8.2 us
    all_to_all x1, starting transfers between devices, from_everyone(): lax.all_to_all(jnp.broadcast_to(shard[None], (size, *shard.shape)), axis,...  3.88 us
  transfers between devices with their start and end apart: 1, of which 1 were waited for; matrix products, arithmetic and copies ran while one was open for 1% of the time, Pallas kernels for 0%

commit v1 on v0

v1 whole, which is shorter than its diff:
```python
import functools

import jax
import jax.numpy as jnp
from jax import lax
from jax.experimental import pallas as pl
from jax.experimental.pallas import tpu as pltpu
from jax.sharding import Mesh
from jax.sharding import PartitionSpec as P

NS_STEPS = 5
LANES = 128
ROWS = 512
HALF = ROWS // 2
MESH = pl.DeviceIdType.MESH
F32, BF16 = jnp.float32, jnp.bfloat16


def dot(a, b):
    return jnp.dot(a, b, preferred_element_type=F32)


def dot_nt(a, b):
    return lax.dot_general(a, b, (((1,), (1,)), ((), ())), preferred_element_type=F32)


def split(a):
    high = a.astype(BF16)
    return high, (a - high.astype(F32)).astype(BF16)


def dot3(a, b):
    ah, al = a
    bh, bl = b
    return dot(ah, bh) + (dot(ah, bl) + dot(al, bh))


def kernel(
    sizes,
    subjects,
    data_hbm,
    maps_hbm,
    resp_hbm,
    new_hbm,
    d,
    end,
    w,
    part_r,
    part_c,
    pair_r,
    pair_c,
    sum_r,
    sum_c,
    r1,
    c1,
    r2,
    c2,
    r2_sum,
    c2_sum,
    swap,
    full_r,
    full_c,
    gram_hi,
    gram_lo,
    a_hi,
    a_lo,
    resp,
    new,
    local_sem,
    send_sem,
    recv_sem,
):
    nz, ny, nx = sizes
    trs = data_hbm.shape[1]
    me = {name: lax.axis_index(name) for name in ("subj", "y", "x", "core")}
    size = {"subj": nz, "y": ny, "x": nx, "core": 2}
    core = me["core"]
    other = 1 - core

    edge = trs // 16 * 16
    load_d = pltpu.make_async_copy(
        data_hbm.at[0, pl.ds(0, edge)], d.at[pl.ds(0, edge)], local_sem.at[0]
    )
    load_end = pltpu.make_async_copy(
        data_hbm.at[0, pl.ds(edge, trs - edge)], end, local_sem.at[2]
    )
    load_end.start()
    load_w = pltpu.make_async_copy(maps_hbm.at[0], w, local_sem.at[1])
    load_d.start()
    load_w.start()

    barrier = pltpu.get_barrier_semaphore()
    partners = 0
    for axis, n in size.items():
        for s in range(1, n):
            pl.semaphore_signal(
                barrier,
                inc=1,
                device_id={axis: lax.rem(me[axis] + s, n)},
                device_id_type=MESH,
            )
            partners += 1

    pending = []

    def send(src, dst, axis, s, arrived):
        k = len(pending)
        copy = pltpu.make_async_remote_copy(
            src_ref=src,
            dst_ref=dst,
            send_sem=send_sem.at[k],
            recv_sem=recv_sem.at[k],
            device_id={axis: lax.rem(me[axis] + s, size[axis])},
            device_id_type=MESH,
        )
        copy.start()
        pending.append(copy)
        back = pltpu.make_async_remote_copy(
            src_ref=src,
            dst_ref=arrived,
            send_sem=send_sem.at[k],
            recv_sem=recv_sem.at[k],
            device_id={axis: lax.rem(me[axis] + s, size[axis])},
            device_id_type=MESH,
        )
        return back.wait_recv

    def near_first(n):
        return sorted(range(1, n), key=lambda s: min(s, n - s))

    def far_first(n):
        return near_first(n)[::-1]

    def ahead(axis, s):
        return lax.rem(me[axis] + s, size[axis])

    def behind(axis, s):
        return lax.rem(me[axis] + (size[axis] - s), size[axis])

    def rows(start, count):
        return pl.ds(pl.multiple_of(start, 8), count)

    zeros = jnp.zeros((LANES, LANES), F32)
    for slot in range(4):
        part_c[1, pl.ds(slot * LANES, LANES)] = zeros
    load_end.wait()
    d[pl.ds(edge, ROWS - edge), :] = jnp.concatenate(
        [end[...], jnp.zeros((ROWS - trs, d.shape[1]), BF16)], axis=0
    )
    load_d.wait()
    load_w.wait()
    partial = dot_nt(d[...], w[...])
    part_r[0] = partial[:, :LANES]
    part_r[1] = partial[:, LANES:]
    pl.semaphore_wait(barrier, partners)
    got_pair_r = send(part_r.at[other], pair_r, "core", 1, pair_r)

    row = lax.broadcasted_iota(jnp.int32, (LANES, LANES), 0)
    col = lax.broadcasted_iota(jnp.int32, (LANES, LANES), 1)
    top = dot_nt(d[pl.ds(0, HALF), :], d[pl.ds(0, HALF), :])
    c00, c10, c11 = top[:LANES, :LANES], top[LANES:, :LANES], top[LANES:, LANES:]
    part_c[0, pl.ds(0, LANES)] = c10
    part_c[0, pl.ds(3 * LANES, LANES)] = jnp.where(row >= col, c00, c11)
    low = dot_nt(d[pl.ds(HALF, HALF), :], d[...])
    part_c[0, pl.ds(LANES, LANES)] = low[:LANES, :LANES]
    part_c[0, pl.ds(2 * LANES, LANES)] = low[:LANES, LANES : 2 * LANES]
    c22 = low[:LANES, 2 * LANES : 3 * LANES]
    c33 = low[LANES:, 3 * LANES :]
    last = 72
    for slot in range(3):
        part_c[1, pl.ds(slot * LANES, last)] = low[
            LANES : LANES + last, slot * LANES : (slot + 1) * LANES
        ]
    part_c[1, pl.ds(3 * LANES, LANES)] = jnp.where(row >= col, c22, c33)
    on_diagonal = row == col
    for slot, block in ((0, c11), (1, c33)):
        diagonal = jnp.sum(jnp.where(on_diagonal, block, 0.0), axis=0, keepdims=True)
        part_c[1, pl.ds(slot * LANES + 80, 8)] = jnp.broadcast_to(diagonal, (8, LANES))
    got_pair_c = send(part_c.at[other], pair_c, "core", 1, pair_c)

    lanes_of = (("subj", "y", 0), ("y", "subj", 1))
    got_pair_r()
    sum_r[...] = part_r[core] + pair_r[...]
    got = {}
    for axis, _, half in lanes_of:
        n = size[axis]
        block = HALF // n
        for s in far_first(n):
            got[half, s] = send(
                sum_r.at[rows(half * HALF + ahead(axis, s) * block, block)],
                r1.at[half, s - 1, pl.ds(0, block)],
                axis,
                s,
                r1.at[half, s - 1, pl.ds(0, block)],
            )
    got_pair_c()
    sum_c[...] = part_c[core] + pair_c[...]
    block_x = ROWS // nx
    for s in far_first(nx):
        got["c", s] = send(
            sum_c.at[rows(ahead("x", s) * block_x, block_x)], c1.at[s - 1], "x", s, c1.at[s - 1]
        )
    for axis, _, half in lanes_of:
        n = size[axis]
        block = HALF // n
        fine = block // nx
        total = sum_r[rows(half * HALF + me[axis] * block, block)]
        for s in near_first(n):
            got[half, s]()
            total = total + r1[half, s - 1, pl.ds(0, block)]
        r2_sum[half, pl.ds(0, block)] = total
        for s in far_first(nx):
            got[half, "x", s] = send(
                r2_sum.at[half, rows(ahead("x", s) * fine, fine)],
                r2.at[half, s - 1, pl.ds(0, fine)],
                "x",
                s,
                r2.at[half, s - 1, pl.ds(0, fine)],
            )
    total = sum_c[rows(me["x"] * block_x, block_x)]
    for s in near_first(nx):
        got["c", s]()
        total = total + c1[s - 1]
    c2_sum[...] = total
    fine_c = block_x // ny
    for s in far_first(ny):
        got["c", "y", s] = send(
            c2_sum.at[rows(ahead("y", s) * fine_c, fine_c)], c2.at[s - 1], "y", s, c2.at[s - 1]
        )
    for axis, across, half in lanes_of:
        fine = HALF // size[axis] // nx
        n = size[across]
        total = r2_sum[half, rows(me["x"] * fine, fine)]
        for s in near_first(nx):
            got[half, "x", s]()
            total = total + r2[half, s - 1, pl.ds(0, fine)]
        swap[half, me[across], pl.ds(0, fine)] = total
        for s in far_first(n):
            got[half, "swap", s] = send(
                swap.at[half, me[across], pl.ds(0, fine)],
                swap.at[half, me[across], pl.ds(0, fine)],
                across,
                s,
                swap.at[half, behind(across, s), pl.ds(0, fine)],
            )
    total = c2_sum[rows(me["y"] * fine_c, fine_c)]
    for s in near_first(ny):
        got["c", "y", s]()
        total = total + c2[s - 1]

    def gram_rows(x, y):
        return rows(x * block_x + y * fine_c, fine_c)

    mine = full_c.at[core, gram_rows(me["x"], me["y"])]
    mine[...] = total
    for s in far_first(ny):
        got["c", "ay", s] = send(
            mine, mine, "y", s, full_c.at[core, gram_rows(me["x"], behind("y", s))]
        )
    for axis, across, half in lanes_of:
        block = HALF // size[axis]
        fine = block // nx
        n = size[across]
        for s in near_first(n):
            got[half, "swap", s]()
        total = swap[half, 0, pl.ds(0, fine)]
        for i in range(1, n):
            total = total + swap[half, i, pl.ds(0, fine)]
        start = half * HALF + me[axis] * block
        mine = full_r.at[core, rows(start + me["x"] * fine, fine)]
        mine[...] = total * (1.0 / subjects)
        for s in far_first(nx):
            got[half, "ax", s] = send(
                mine, mine, "x", s, full_r.at[core, rows(start + behind("x", s) * fine, fine)]
            )
    for s in near_first(ny):
        got["c", "ay", s]()
    got_other = []
    mine = full_c.at[core, rows(me["x"] * block_x, block_x)]
    for s in far_first(nx):
        got["c", "ax", s] = send(
            mine, mine, "x", s, full_c.at[core, rows(behind("x", s) * block_x, block_x)]
        )
    got_other_c = [
        send(mine, mine, "core", 1, full_c.at[other, rows(me["x"] * block_x, block_x)])
    ]
    got_other_r = []
    for axis, _, half in lanes_of:
        n = size[axis]
        block = HALF // n
        for s in near_first(nx):
            got[half, "ax", s]()
        here = rows(half * HALF + me[axis] * block, block)
        mine = full_r.at[core, here]
        for s in far_first(n):
            there = rows(half * HALF + behind(axis, s) * block, block)
            got[half, "az", s] = send(mine, mine, axis, s, full_r.at[core, there])
        got_other_r.append(send(mine, mine, "core", 1, full_r.at[other, here]))
    for s in near_first(nx):
        got["c", "ax", s]()
        here = rows(behind("x", s) * block_x, block_x)
        mine = full_c.at[core, here]
        got_other_c.append(send(mine, mine, "core", 1, full_c.at[other, here]))

    def forward(hops):
        for axis, _, half in lanes_of:
            n = size[axis]
            block = HALF // n
            for s in near_first(n):
                if (min(s, n - s) <= 2) != hops:
                    continue
                got[half, "az", s]()
                here = rows(half * HALF + behind(axis, s) * block, block)
                mine = full_r.at[core, here]
                got_other_r.append(send(mine, mine, "core", 1, full_r.at[other, here]))

    forward(True)
    for wait in got_other_c:
        wait()

    def put(i, j, block):
        high, low_part = split(block)
        gram_hi[pl.ds(i * LANES, LANES), pl.ds(j * LANES, LANES)] = high
        gram_lo[pl.ds(i * LANES, LANES), pl.ds(j * LANES, LANES)] = low_part

    def put_both(i, j, block):
        put(i, j, block)
        put(j, i, block.T)

    put_both(1, 0, full_c[0, pl.ds(0, LANES)])
    put_both(2, 0, full_c[0, pl.ds(LANES, LANES)])
    put_both(2, 1, full_c[0, pl.ds(2 * LANES, LANES)])
    for slot in range(3):
        block = full_c[1, pl.ds(slot * LANES, LANES)]
        put_both(3, slot, jnp.where(row < last, block, 0.0))
    for half, i, j in ((0, 0, 1), (1, 2, 3)):
        packed = full_c[half, pl.ds(3 * LANES, LANES)]
        turned = packed.T
        diagonal = full_c[1, pl.ds(half * LANES + 80, 8)][:1]
        put(i, i, jnp.where(row >= col, packed, turned))
        block = jnp.where(row < col, packed, turned)
        put(j, j, jnp.where(on_diagonal, jnp.broadcast_to(diagonal, block.shape), block))

    forward(False)
    for wait in got_other_r:
        wait()

    response = jnp.concatenate([full_r[0], full_r[1]], axis=1)
    resp[...] = response[:trs]
    store_r = pltpu.make_async_copy(resp, resp_hbm, local_sem.at[0])
    store_r.start()
    shared = response.astype(BF16)
    shared_t = shared.T
    t = dot(shared_t, gram_hi[...]) + dot(shared_t, gram_lo[...])
    t_hi, t_lo = split(t)
    gram = dot(t_hi, shared) + dot(t_lo, shared)
    k = gram.shape[0]

    scale = jnp.sqrt(jnp.sum(gram * gram, keepdims=True) + 1e-06)
    estimate = gram / scale
    unit = lax.broadcasted_iota(jnp.int32, (k, k), 0) == lax.broadcasted_iota(
        jnp.int32, (k, k), 1
    )
    eye = jnp.where(unit, 1.5, 0.0).astype(F32)
    middle = split(eye - 0.5 * estimate)
    inverse = middle
    estimate = split(dot3(split(estimate), middle))
    a = dot(shared_t, d[...])
    a_hi[...], a_lo[...] = split(a)
    for step in range(1, NS_STEPS):
        middle = split(eye - 0.5 * dot3(inverse, estimate))
        inverse = split(dot3(middle, inverse))
        if step < NS_STEPS - 1:
            estimate = split(dot3(estimate, middle))
    root = 1.0 / jnp.sqrt(scale)
    stores = []
    width = 256
    for i in range(new.shape[1] // width):
        part = pl.ds(i * width, width)
        out = dot3(inverse, (a_hi[:, part], a_lo[:, part])) * root
        new[:, part] = out.astype(BF16)
        store = pltpu.make_async_copy(
            new.at[:, part], new_hbm.at[0, :, part], local_sem.at[1 + i]
        )
        store.start()
        stores.append(store)
    for copy in pending:
        copy.wait_send()
    for store in stores:
        store.wait()
    store_r.wait()


def solution(mesh):
    nz, ny, nx = mesh.shape["subj"], 8, 4
    names = ("subj", "y", "x", "core")
    return build(Mesh(mesh.devices.reshape(nz, ny, nx, 2), names))


def build(grid):
    vox = ("y", "x", "core")
    nz, ny, nx = (grid.shape[name] for name in ("subj", "y", "x"))
    block_z, block_y = HALF // nz, HALF // ny
    block = max(block_z, block_y)
    block_x = ROWS // nx
    copies = 4 + 3 * (nz - 1) + 3 * (ny - 1) + 6 * (nx - 1) + 2 * (ny - 1) + 4 * nx + 2 * (nz + ny)

    def shards(data, maps):
        _, trs, vectors = data.shape
        k = maps.shape[1]
        subjects = nz * data.shape[0]
        vmem = pltpu.VMEM
        response, new_maps = pl.pallas_call(
            functools.partial(kernel, (nz, ny, nx), subjects),
            name="srm_step",
            out_shape=(
                jax.ShapeDtypeStruct((trs, k), F32),
                jax.ShapeDtypeStruct((1, k, vectors), BF16),
            ),
            in_specs=[pl.BlockSpec(memory_space=pl.ANY)] * 2,
            out_specs=[pl.BlockSpec(memory_space=pl.ANY)] * 2,
            scratch_shapes=[
                vmem((ROWS, vectors), BF16),
                vmem((trs % 16, vectors), BF16),
                vmem((k, vectors), BF16),
                vmem((2, ROWS, LANES), F32),
                vmem((2, ROWS, LANES), F32),
                vmem((ROWS, LANES), F32),
                vmem((ROWS, LANES), F32),
                vmem((ROWS, LANES), F32),
                vmem((ROWS, LANES), F32),
                vmem((2, max(nz, ny) - 1, block, LANES), F32),
                vmem((nx - 1, block_x, LANES), F32),
                vmem((2, nx - 1, block // nx, LANES), F32),
                vmem((ny - 1, block_x // ny, LANES), F32),
                vmem((2, block, LANES), F32),
                vmem((block_x, LANES), F32),
                vmem((2, max(nz, ny), block // nx, LANES), F32),
                vmem((2, ROWS, LANES), F32),
                vmem((2, ROWS, LANES), F32),
                vmem((ROWS, ROWS), BF16),
                vmem((ROWS, ROWS), BF16),
                vmem((k, vectors), BF16),
                vmem((k, vectors), BF16),
                vmem((trs, k), F32),
                vmem((k, vectors), BF16),
                pltpu.SemaphoreType.DMA((8,)),
                pltpu.SemaphoreType.DMA((copies,)),
                pltpu.SemaphoreType.DMA((copies,)),
            ],
            compiler_params=pltpu.CompilerParams(
                collective_id=0, has_side_effects=True, vmem_limit_bytes=48 << 20
            ),
        )(data, maps)
        return response, new_maps

    return jax.shard_map(
        shards,
        mesh=grid,
        in_specs=(P("subj", None, vox), P("subj", None, vox)),
        out_specs=(P(), P("subj", None, vox)),
        check_vma=False,
    )
```

time: 123 us -> 53.1 us (0.43)
  blocking collectives: 93.5 us -> 0 us
  Pallas kernels: 0 us -> 48.5 us
  matrix products: 10.6 us -> 0 us
  waiting for transfers between devices: 8.2 us -> 0 us
  starting transfers between devices: 3.88 us -> 0 us
    all_to_all x7 -> x0, blocking collectives: 93.5 us -> none  [the longest x3 49.2 us: from_everyone(): lax.all_to_all(jnp.broadcast_to(shard[None], (size, *shard.shape)), axis,...]
    pallas_call x0 -> x1, Pallas kernels: none -> 48.5 us  [shards(): pl.pallas_call(functools.partial(kernel, (nz, ny, nx), subjects), name='s...]
    dot_general x18 -> x0, matrix products: 10.6 us -> none  [the longest x1 1.83 us: shards(): jnp.einsum('czm,cmj->czj', subject_factor, projected_signal, precision=la...]
    all_to_all x1 -> x0, waiting for transfers between devices: 8.2 us -> none  [from_everyone(): lax.all_to_all(jnp.broadcast_to(shard[None], (size, *shard.shape)), axis,...]
    all_to_all x1 -> x0, starting transfers between devices: 3.88 us -> none  [from_everyone(): lax.all_to_all(jnp.broadcast_to(shard[None], (size, *shard.shape)), axis,...]
    unnamed x3 -> x6, local copies, waits for them, and re-layouts: 2.14 us -> 3.78 us
  transfers between devices with their start and end apart: 1 -> 0, of which waited for: 1 -> 0; matrix products, arithmetic and copies ran while one was open for 1% -> 0% of each run, Pallas kernels for 0% -> 0%
where the time goes in v1:
time: 53.1 us; the launch traced here: 52.9 us
  Pallas kernels  48.5 us (91%)
  local copies, waits for them, and re-layouts  3.78 us (7%)
  between operations  0.65 us (1%)
    pallas_call x1, Pallas kernels, shards(): pl.pallas_call(functools.partial(kernel, (nz, ny, nx), subjects), name='s...  48.5 us
    unnamed x6, local copies, waits for them, and re-layouts  3.78 us

profile of v1, /device:TPU:1, one launch (start us, length us, event | category | flops | bytes accessed | tf_op | source)
XLA Modules:
  0.0 52.9 jit_solution(311513044154047388)
XLA Ops:
  0.6 0.0 copy-start
  0.6 1.2 %copy-done = bf16[1,450,1024]{2,1,0:T(8,128)(2,1)S(1)} copy-done((bf16[1,450,1024]{2,1,0:T(8,128)(2,1)S(1)}, bf16[1,450,1024]{2,1,0:T(8,128)(2,1)}, u32[]{:S(2)}) %copy-start) | copy-done | bytes 921624
  1.8 0.0 copy-start.1
  1.8 1.0 %copy-done.1 = bf16[1,256,1024]{2,1,0:T(8,128)(2,1)S(1)} copy-done((bf16[1,256,1024]{2,1,0:T(8,128)(2,1)S(1)}, bf16[1,256,1024]{2,1,0:T(8,128)(2,1)}, u32[]{:S(2)}) %copy-start.1) | copy-done | bytes 524312
  2.9 48.5 %srm_step.1 = (f32[450,256]{1,0:T(8,128)S(1)}, bf16[1,256,1024]{2,1,0:T(8,128)(2,1)S(1)}) custom-call(bf16[1,450,1024]{2,1,0:T(8,128)(2,1)S(1)} %copy-done, bf16[1,256,1024]{2,1,0:T(8,128)(2,1)S(1)} %copy-done.1), custom_call_target="tpu_custom_call" | custom-call | tf_op jit(solution)/shard_map/srm_step/pallas_call | solution.py:413
  51.3 0.8 %copy.6 = f32[450,256]{1,0:T(8,128)} copy(f32[450,256]{1,0:T(8,128)S(1)} %get-tuple-element.4) | data formatting | bytes 921600
  52.1 0.8 %copy.7 = bf16[1,256,1024]{2,1,0:T(8,128)(2,1)} copy(bf16[1,256,1024]{2,1,0:T(8,128)(2,1)S(1)} %get-tuple-element.5) | data formatting | bytes 1048576
Async XLA Ops:
  0.6 1.2 %copy-start = (bf16[1,450,1024]{2,1,0:T(8,128)(2,1)S(1)}, bf16[1,450,1024]{2,1,0:T(8,128)(2,1)}, u32[]{:S(2)}) copy-start(bf16[1,450,1024]{2,1,0:T(8,128)(2,1)} %data_hbm.1) | copy-start | bytes 2764804
  1.8 1.0 %copy-start.1 = (bf16[1,256,1024]{2,1,0:T(8,128)(2,1)S(1)}, bf16[1,256,1024]{2,1,0:T(8,128)(2,1)}, u32[]{:S(2)}) copy-start(bf16[1,256,1024]{2,1,0:T(8,128)(2,1)} %maps_hbm.1) | copy-start | bytes 1572868

commit v2 on v1

--- a/solution.py
+++ b/solution.py
@@ -11,6 +11,7 @@
 NS_STEPS = 5
 LANES = 128
 ROWS = 512
+CHUNKS = 2
 HALF = ROWS // 2
 MESH = pl.DeviceIdType.MESH
 F32, BF16 = jnp.float32, jnp.bfloat16
@@ -40,8 +41,11 @@
     subjects,
     data_hbm,
     maps_hbm,
-    resp_hbm,
-    new_hbm,
+    p_hi,
+    p_lo,
+    a_hi,
+    a_lo,
+    resp,
     d,
     end,
     w,
@@ -62,10 +66,6 @@
     full_c,
     gram_hi,
     gram_lo,
-    a_hi,
-    a_lo,
-    resp,
-    new,
     local_sem,
     send_sem,
     recv_sem,
@@ -78,16 +78,23 @@
     other = 1 - core
 
     edge = trs // 16 * 16
-    load_d = pltpu.make_async_copy(
-        data_hbm.at[0, pl.ds(0, edge)], d.at[pl.ds(0, edge)], local_sem.at[0]
-    )
+    chunk = d.shape[1] // CHUNKS
     load_end = pltpu.make_async_copy(
-        data_hbm.at[0, pl.ds(edge, trs - edge)], end, local_sem.at[2]
+        data_hbm.at[0, pl.ds(edge, trs - edge)], end, local_sem.at[2 * CHUNKS]
     )
     load_end.start()
-    load_w = pltpu.make_async_copy(maps_hbm.at[0], w, local_sem.at[1])
-    load_d.start()
-    load_w.start()
+    loads = []
+    for i in range(CHUNKS):
+        part = pl.ds(i * chunk, chunk)
+        load_d = pltpu.make_async_copy(
+            data_hbm.at[0, pl.ds(0, edge), part], d.at[pl.ds(0, edge), part], local_sem.at[2 * i]
+        )
+        load_w = pltpu.make_async_copy(
+            maps_hbm.at[0, :, part], w.at[:, part], local_sem.at[2 * i + 1]
+        )
+        load_d.start()
+        load_w.start()
+        loads.append((part, load_d, load_w))
 
     barrier = pltpu.get_barrier_semaphore()
     partners = 0
@@ -147,9 +154,12 @@
     d[pl.ds(edge, ROWS - edge), :] = jnp.concatenate(
         [end[...], jnp.zeros((ROWS - trs, d.shape[1]), BF16)], axis=0
     )
-    load_d.wait()
-    load_w.wait()
-    partial = dot_nt(d[...], w[...])
+    partial = None
+    for part, load_d, load_w in loads:
+        load_d.wait()
+        load_w.wait()
+        term = dot_nt(d[:, part], w[:, part])
+        partial = term if partial is None else partial + term
     part_r[0] = partial[:, :LANES]
     part_r[1] = partial[:, LANES:]
     pl.semaphore_wait(barrier, partners)
@@ -275,7 +285,6 @@
             )
     for s in near_first(ny):
         got["c", "ay", s]()
-    got_other = []
     mine = full_c.at[core, rows(me["x"] * block_x, block_x)]
     for s in far_first(nx):
         got["c", "ax", s] = send(
@@ -302,19 +311,16 @@
         mine = full_c.at[core, here]
         got_other_c.append(send(mine, mine, "core", 1, full_c.at[other, here]))
 
-    def forward(hops):
+    for s in near_first(max(nz, ny)):
         for axis, _, half in lanes_of:
             n = size[axis]
+            if s >= n:
+                continue
             block = HALF // n
-            for s in near_first(n):
-                if (min(s, n - s) <= 2) != hops:
-                    continue
-                got[half, "az", s]()
-                here = rows(half * HALF + behind(axis, s) * block, block)
-                mine = full_r.at[core, here]
-                got_other_r.append(send(mine, mine, "core", 1, full_r.at[other, here]))
-
-    forward(True)
+            got[half, "az", s]()
+            here = rows(half * HALF + behind(axis, s) * block, block)
+            mine = full_r.at[core, here]
+            got_other_r.append(send(mine, mine, "core", 1, full_r.at[other, here]))
     for wait in got_other_c:
         wait()
 
@@ -341,18 +347,14 @@
         block = jnp.where(row < col, packed, turned)
         put(j, j, jnp.where(on_diagonal, jnp.broadcast_to(diagonal, block.shape), block))
 
-    forward(False)
     for wait in got_other_r:
         wait()
 
     response = jnp.concatenate([full_r[0], full_r[1]], axis=1)
     resp[...] = response[:trs]
-    store_r = pltpu.make_async_copy(resp, resp_hbm, local_sem.at[0])
-    store_r.start()
     shared = response.astype(BF16)
     shared_t = shared.T
-    t = dot(shared_t, gram_hi[...]) + dot(shared_t, gram_lo[...])
-    t_hi, t_lo = split(t)
+    t_hi, t_lo = split(dot(shared_t, gram_hi[...]) + dot(shared_t, gram_lo[...]))
     gram = dot(t_hi, shared) + dot(t_lo, shared)
     k = gram.shape[0]
 
@@ -362,30 +364,32 @@
         jnp.int32, (k, k), 1
     )
     eye = jnp.where(unit, 1.5, 0.0).astype(F32)
-    middle = split(eye - 0.5 * estimate)
-    inverse = middle
-    estimate = split(dot3(split(estimate), middle))
-    a = dot(shared_t, d[...])
-    a_hi[...], a_lo[...] = split(a)
+    middle = eye - 0.5 * estimate
+    both = jnp.concatenate([dot3(split(estimate), split(middle)), middle], axis=0)
+    a_hi[...], a_lo[...] = split(dot(shared_t, d[...]))
     for step in range(1, NS_STEPS):
-        middle = split(eye - 0.5 * dot3(inverse, estimate))
-        inverse = split(dot3(middle, inverse))
+        high, low_part = split(both)
+        inverse = (high[k:], low_part[k:])
+        middle = split(eye - 0.5 * dot3(inverse, (high[:k], low_part[:k])))
         if step < NS_STEPS - 1:
-            estimate = split(dot3(estimate, middle))
-    root = 1.0 / jnp.sqrt(scale)
+            both = dot3((high, low_part), middle)
+    p_hi[...], p_lo[...] = split(dot3(inverse, middle) * (1.0 / jnp.sqrt(scale)))
+    for copy in pending:
+        copy.wait_send()
+
+
+def finish(p_hi, p_lo, a_hi, a_lo, resp, resp_hbm, new_hbm, new, sem):
+    store_r = pltpu.make_async_copy(resp, resp_hbm, sem.at[0])
+    store_r.start()
     stores = []
     width = 256
     for i in range(new.shape[1] // width):
         part = pl.ds(i * width, width)
-        out = dot3(inverse, (a_hi[:, part], a_lo[:, part])) * root
+        out = dot3((p_hi[...], p_lo[...]), (a_hi[:, part], a_lo[:, part]))
         new[:, part] = out.astype(BF16)
-        store = pltpu.make_async_copy(
-            new.at[:, part], new_hbm.at[0, :, part], local_sem.at[1 + i]
-        )
+        store = pltpu.make_async_copy(new.at[:, part], new_hbm.at[0, :, part], sem.at[1 + i])
         store.start()
         stores.append(store)
-    for copy in pending:
-        copy.wait_send()
     for store in stores:
         store.wait()
     store_r.wait()
@@ -410,15 +414,20 @@
         k = maps.shape[1]
         subjects = nz * data.shape[0]
         vmem = pltpu.VMEM
-        response, new_maps = pl.pallas_call(
+        held = pl.BlockSpec(memory_space=pltpu.VMEM)
+        hbm = pl.BlockSpec(memory_space=pltpu.HBM)
+        parts = pl.pallas_call(
             functools.partial(kernel, (nz, ny, nx), subjects),
             name="srm_step",
             out_shape=(
+                jax.ShapeDtypeStruct((k, k), BF16),
+                jax.ShapeDtypeStruct((k, k), BF16),
+                jax.ShapeDtypeStruct((k, vectors), BF16),
+                jax.ShapeDtypeStruct((k, vectors), BF16),
                 jax.ShapeDtypeStruct((trs, k), F32),
-                jax.ShapeDtypeStruct((1, k, vectors), BF16),
             ),
-            in_specs=[pl.BlockSpec(memory_space=pl.ANY)] * 2,
-            out_specs=[pl.BlockSpec(memory_space=pl.ANY)] * 2,
+            in_specs=[hbm] * 2,
+            out_specs=[held] * 5,
             scratch_shapes=[
                 vmem((ROWS, vectors), BF16),
                 vmem((trs % 16, vectors), BF16),
@@ -440,19 +449,26 @@
                 vmem((2, ROWS, LANES), F32),
                 vmem((ROWS, ROWS), BF16),
                 vmem((ROWS, ROWS), BF16),
-                vmem((k, vectors), BF16),
-                vmem((k, vectors), BF16),
-                vmem((trs, k), F32),
-                vmem((k, vectors), BF16),
-                pltpu.SemaphoreType.DMA((8,)),
+                pltpu.SemaphoreType.DMA((2 * CHUNKS + 1,)),
                 pltpu.SemaphoreType.DMA((copies,)),
                 pltpu.SemaphoreType.DMA((copies,)),
             ],
             compiler_params=pltpu.CompilerParams(
-                collective_id=0, has_side_effects=True, vmem_limit_bytes=48 << 20
+                collective_id=0, has_side_effects=True, vmem_limit_bytes=54_550_000
             ),
         )(data, maps)
-        return response, new_maps
+        return pl.pallas_call(
+            finish,
+            name="srm_maps",
+            out_shape=(
+                jax.ShapeDtypeStruct((trs, k), F32),
+                jax.ShapeDtypeStruct((1, k, vectors), BF16),
+            ),
+            in_specs=[held] * 5,
+            out_specs=[hbm] * 2,
+            scratch_shapes=[vmem((k, vectors), BF16), pltpu.SemaphoreType.DMA((8,))],
+            compiler_params=pltpu.CompilerParams(vmem_limit_bytes=16 << 20),
+        )(*parts)
 
     return jax.shard_map(
         shards,

time: 53.1 us -> 49.4 us (0.930)
  local copies, waits for them, and re-layouts: 3.78 us -> 0 us
    unnamed x6 -> x0, local copies, waits for them, and re-layouts: 3.78 us -> none
    pallas_call x0 -> x1, Pallas kernels: none -> 1.36 us  [shards(): pl.pallas_call(finish, name='srm_maps', out_shape=(jax.ShapeDtypeStruct((...]
    pallas_call x1, Pallas kernels: 48.5 us -> 47.3 us  [shards(): pl.pallas_call(functools.partial(kernel, (nz, ny, nx), subjects), name='s...]
where the time goes in v2:
time: 49.4 us; the launch traced here: 49.2 us
  Pallas kernels  48.6 us (98%)
  between operations  0.64 us (1%)
    pallas_call x1, Pallas kernels, shards(): pl.pallas_call(functools.partial(kernel, (nz, ny, nx), subjects), name='s...  47.3 us
    pallas_call x1, Pallas kernels, shards(): pl.pallas_call(finish, name='srm_maps', out_shape=(jax.ShapeDtypeStruct((...  1.36 us

profile of v2, /device:TPU:1, one launch (start us, length us, event | category | flops | bytes accessed | tf_op | source)
XLA Modules:
  0.0 49.2 jit_solution(16276344859546865512)
XLA Ops:
  0.6 47.3 %srm_step.1 = (bf16[256,256]{1,0:T(8,128)(2,1)S(1)}, bf16[256,256]{1,0:T(8,128)(2,1)S(1)}, bf16[256,1024]{1,0:T(8,128)(2,1)S(1)}, bf16[256,1024]{1,0:T(8,128)(2,1)S(1)}, f32[450,256]{1,0:T(8,128)S(1)}) custom-call(bf16[1,450,1024]{2,1,0:T(8,128)(2,1)} %data_hbm.1, bf16[1,256,1024]{2,1,0:T(8,128)(2,1)} %maps_hbm.1), custom_call_target="tpu_custom_call" | custom-call | tf_op jit(solution)/shard_map/srm_step/pallas_call | solution.py:419
  47.9 1.4 %srm_maps.1 = (f32[450,256]{1,0:T(8,128)}, bf16[1,256,1024]{2,1,0:T(8,128)(2,1)}) custom-call(bf16[256,256]{1,0:T(8,128)(2,1)S(1)} %get-tuple-element.7.p_hi, bf16[256,256]{1,0:T(8,128)(2,1)S(1)} %get-tuple-element.8.p_lo, bf16[256,1024]{1,0:T(8,128)(2,1)S(1)} %get-tuple-element.9.a_hi, bf16[256,1024]{1,0:T(8,128)(2,1)S(1)} %get-tuple-element.10.a_lo, ...), custom_call_target="tpu_custom_call" | custom-call | tf_op jit(solution)/shard_map/srm_maps/pallas_call | solution.py:460

commit v3 on v2

--- a/solution.py
+++ b/solution.py
@@ -12,7 +12,15 @@
 LANES = 128
 ROWS = 512
 CHUNKS = 2
+LAG = 4
 HALF = ROWS // 2
+C_X = 256
+SUMS = (
+    ("r", 0, HALF, "subj", ("x", "y")),
+    ("r", HALF, HALF, "y", ("x", "subj")),
+    ("c", 0, C_X, "x", ("y",)),
+    ("c", C_X, ROWS - C_X, "y", ("x",)),
+)
 MESH = pl.DeviceIdType.MESH
 F32, BF16 = jnp.float32, jnp.bfloat16
 
@@ -55,13 +63,6 @@
     pair_c,
     sum_r,
     sum_c,
-    r1,
-    c1,
-    r2,
-    c2,
-    r2_sum,
-    c2_sum,
-    swap,
     full_r,
     full_c,
     gram_hi,
@@ -69,6 +70,7 @@
     local_sem,
     send_sem,
     recv_sem,
+    *buffers,
 ):
     nz, ny, nx = sizes
     trs = data_hbm.shape[1]
@@ -131,6 +133,9 @@
             device_id_type=MESH,
         )
         return back.wait_recv
+
+    def nosend(*a):
+        return lambda: None
 
     def near_first(n):
         return sorted(range(1, n), key=lambda s: min(s, n - s))
@@ -188,140 +193,90 @@
         part_c[1, pl.ds(slot * LANES + 80, 8)] = jnp.broadcast_to(diagonal, (8, LANES))
     got_pair_c = send(part_c.at[other], pair_c, "core", 1, pair_c)
 
-    lanes_of = (("subj", "y", 0), ("y", "subj", 1))
+    got_other = {"r": [], "c": []}
+
+    def summed(name, source, full, factor, start, count, axis, others, buffers):
+        n = size[axis]
+        block = count // n
+        arrived, *swaps = buffers
+        got = {}
+
+        def place(at):
+            return rows(start + at * block, block)
+
+        for s in far_first(n):
+            slot = arrived.at[s - 1]
+            got[s] = send(source.at[place(ahead(axis, s))], slot, axis, s, slot)
+        yield
+        total = source[place(me[axis])]
+        for s in far_first(n):
+            got[s]()
+            total = total + arrived[s - 1]
+        for across, swap in zip(others, swaps):
+            m = size[across]
+            mine = swap.at[me[across]]
+            mine[...] = total
+            for s in far_first(m):
+                got[s] = send(mine, mine, across, s, swap.at[behind(across, s)])
+            yield
+            for s in far_first(m):
+                got[s]()
+            total = swap[0]
+            for i in range(1, m):
+                total = total + swap[i]
+        mine = full.at[core, place(me[axis])]
+        mine[...] = total * factor
+        for s in far_first(n):
+            got[s] = send(mine, mine, axis, s, full.at[core, place(behind(axis, s))])
+        yield
+        for s in far_first(n):
+            got[s]()
+        here = rows(start, count)
+        mine = full.at[core, here]
+        got_other[name].append(send(mine, mine, "core", 1, full.at[other, here]))
+        yield
+
+    marks = []
+    drained = 0
+
+    def drain(upto):
+        nonlocal drained
+        for copy in pending[drained:upto]:
+            copy.wait_send()
+        drained = max(drained, upto)
+
+    def step(*chains):
+        for chain in chains:
+            next(chain)
+        marks.append(len(pending))
+        if len(marks) > LAG:
+            drain(marks[-1 - LAG])
+
+    rest = iter(buffers)
+    chains = []
+    for name, start, count, axis, others in SUMS:
+        source, full, factor = (
+            (sum_r, full_r, 1.0 / subjects) if name == "r" else (sum_c, full_c, 1.0)
+        )
+        own = [next(rest) for _ in range(1 + len(others))]
+        chains.append(summed(name, source, full, factor, start, count, axis, others, own))
+    r0, r1, c0, c1 = chains
     got_pair_r()
     sum_r[...] = part_r[core] + pair_r[...]
-    got = {}
-    for axis, _, half in lanes_of:
-        n = size[axis]
-        block = HALF // n
-        for s in far_first(n):
-            got[half, s] = send(
-                sum_r.at[rows(half * HALF + ahead(axis, s) * block, block)],
-                r1.at[half, s - 1, pl.ds(0, block)],
-                axis,
-                s,
-                r1.at[half, s - 1, pl.ds(0, block)],
-            )
+    step(r0, r1)
     got_pair_c()
     sum_c[...] = part_c[core] + pair_c[...]
-    block_x = ROWS // nx
-    for s in far_first(nx):
-        got["c", s] = send(
-            sum_c.at[rows(ahead("x", s) * block_x, block_x)], c1.at[s - 1], "x", s, c1.at[s - 1]
-        )
-    for axis, _, half in lanes_of:
-        n = size[axis]
-        block = HALF // n
-        fine = block // nx
-        total = sum_r[rows(half * HALF + me[axis] * block, block)]
-        for s in near_first(n):
-            got[half, s]()
-            total = total + r1[half, s - 1, pl.ds(0, block)]
-        r2_sum[half, pl.ds(0, block)] = total
-        for s in far_first(nx):
-            got[half, "x", s] = send(
-                r2_sum.at[half, rows(ahead("x", s) * fine, fine)],
-                r2.at[half, s - 1, pl.ds(0, fine)],
-                "x",
-                s,
-                r2.at[half, s - 1, pl.ds(0, fine)],
-            )
-    total = sum_c[rows(me["x"] * block_x, block_x)]
-    for s in near_first(nx):
-        got["c", s]()
-        total = total + c1[s - 1]
-    c2_sum[...] = total
-    fine_c = block_x // ny
-    for s in far_first(ny):
-        got["c", "y", s] = send(
-            c2_sum.at[rows(ahead("y", s) * fine_c, fine_c)], c2.at[s - 1], "y", s, c2.at[s - 1]
-        )
-    for axis, across, half in lanes_of:
-        fine = HALF // size[axis] // nx
-        n = size[across]
-        total = r2_sum[half, rows(me["x"] * fine, fine)]
-        for s in near_first(nx):
-            got[half, "x", s]()
-            total = total + r2[half, s - 1, pl.ds(0, fine)]
-        swap[half, me[across], pl.ds(0, fine)] = total
-        for s in far_first(n):
-            got[half, "swap", s] = send(
-                swap.at[half, me[across], pl.ds(0, fine)],
-                swap.at[half, me[across], pl.ds(0, fine)],
-                across,
-                s,
-                swap.at[half, behind(across, s), pl.ds(0, fine)],
-            )
-    total = c2_sum[rows(me["y"] * fine_c, fine_c)]
-    for s in near_first(ny):
-        got["c", "y", s]()
-        total = total + c2[s - 1]
-
-    def gram_rows(x, y):
-        return rows(x * block_x + y * fine_c, fine_c)
-
-    mine = full_c.at[core, gram_rows(me["x"], me["y"])]
-    mine[...] = total
-    for s in far_first(ny):
-        got["c", "ay", s] = send(
-            mine, mine, "y", s, full_c.at[core, gram_rows(me["x"], behind("y", s))]
-        )
-    for axis, across, half in lanes_of:
-        block = HALF // size[axis]
-        fine = block // nx
-        n = size[across]
-        for s in near_first(n):
-            got[half, "swap", s]()
-        total = swap[half, 0, pl.ds(0, fine)]
-        for i in range(1, n):
-            total = total + swap[half, i, pl.ds(0, fine)]
-        start = half * HALF + me[axis] * block
-        mine = full_r.at[core, rows(start + me["x"] * fine, fine)]
-        mine[...] = total * (1.0 / subjects)
-        for s in far_first(nx):
-            got[half, "ax", s] = send(
-                mine, mine, "x", s, full_r.at[core, rows(start + behind("x", s) * fine, fine)]
-            )
-    for s in near_first(ny):
-        got["c", "ay", s]()
-    mine = full_c.at[core, rows(me["x"] * block_x, block_x)]
-    for s in far_first(nx):
-        got["c", "ax", s] = send(
-            mine, mine, "x", s, full_c.at[core, rows(behind("x", s) * block_x, block_x)]
-        )
-    got_other_c = [
-        send(mine, mine, "core", 1, full_c.at[other, rows(me["x"] * block_x, block_x)])
-    ]
-    got_other_r = []
-    for axis, _, half in lanes_of:
-        n = size[axis]
-        block = HALF // n
-        for s in near_first(nx):
-            got[half, "ax", s]()
-        here = rows(half * HALF + me[axis] * block, block)
-        mine = full_r.at[core, here]
-        for s in far_first(n):
-            there = rows(half * HALF + behind(axis, s) * block, block)
-            got[half, "az", s] = send(mine, mine, axis, s, full_r.at[core, there])
-        got_other_r.append(send(mine, mine, "core", 1, full_r.at[other, here]))
-    for s in near_first(nx):
-        got["c", "ax", s]()
-        here = rows(behind("x", s) * block_x, block_x)
-        mine = full_c.at[core, here]
-        got_other_c.append(send(mine, mine, "core", 1, full_c.at[other, here]))
-
-    for s in near_first(max(nz, ny)):
-        for axis, _, half in lanes_of:
-            n = size[axis]
-            if s >= n:
-                continue
-            block = HALF // n
-            got[half, "az", s]()
-            here = rows(half * HALF + behind(axis, s) * block, block)
-            mine = full_r.at[core, here]
-            got_other_r.append(send(mine, mine, "core", 1, full_r.at[other, here]))
-    for wait in got_other_c:
+    step(c0, c1)
+    step(c0)
+    step(r0, r1)
+    step(c1)
+    step(r0, r1)
+    step(c1)
+    step(c0)
+    step(r0, r1)
+    step(c0, c1)
+    step(r0, r1)
+    for wait in got_other["c"]:
         wait()
 
     def put(i, j, block):
@@ -347,7 +302,7 @@
         block = jnp.where(row < col, packed, turned)
         put(j, j, jnp.where(on_diagonal, jnp.broadcast_to(diagonal, block.shape), block))
 
-    for wait in got_other_r:
+    for wait in got_other["r"]:
         wait()
 
     response = jnp.concatenate([full_r[0], full_r[1]], axis=1)
@@ -374,8 +329,7 @@
         if step < NS_STEPS - 1:
             both = dot3((high, low_part), middle)
     p_hi[...], p_lo[...] = split(dot3(inverse, middle) * (1.0 / jnp.sqrt(scale)))
-    for copy in pending:
-        copy.wait_send()
+    drain(len(pending))
 
 
 def finish(p_hi, p_lo, a_hi, a_lo, resp, resp_hbm, new_hbm, new, sem):
@@ -404,10 +358,14 @@
 def build(grid):
     vox = ("y", "x", "core")
     nz, ny, nx = (grid.shape[name] for name in ("subj", "y", "x"))
-    block_z, block_y = HALF // nz, HALF // ny
-    block = max(block_z, block_y)
-    block_x = ROWS // nx
-    copies = 4 + 3 * (nz - 1) + 3 * (ny - 1) + 6 * (nx - 1) + 2 * (ny - 1) + 4 * nx + 2 * (nz + ny)
+    size = {"subj": nz, "y": ny, "x": nx}
+    shapes = []
+    copies = 2
+    for _, _, count, axis, others in SUMS:
+        block = count // size[axis]
+        shapes.append((size[axis] - 1, block, LANES))
+        shapes += [(size[across], block, LANES) for across in others]
+        copies += 2 * size[axis] - 1 + sum(size[across] - 1 for across in others)
 
     def shards(data, maps):
         _, trs, vectors = data.shape
@@ -438,13 +396,6 @@
                 vmem((ROWS, LANES), F32),
                 vmem((ROWS, LANES), F32),
                 vmem((ROWS, LANES), F32),
-                vmem((2, max(nz, ny) - 1, block, LANES), F32),
-                vmem((nx - 1, block_x, LANES), F32),
-                vmem((2, nx - 1, block // nx, LANES), F32),
-                vmem((ny - 1, block_x // ny, LANES), F32),
-                vmem((2, block, LANES), F32),
-                vmem((block_x, LANES), F32),
-                vmem((2, max(nz, ny), block // nx, LANES), F32),
                 vmem((2, ROWS, LANES), F32),
                 vmem((2, ROWS, LANES), F32),
                 vmem((ROWS, ROWS), BF16),
@@ -452,6 +403,7 @@
                 pltpu.SemaphoreType.DMA((2 * CHUNKS + 1,)),
                 pltpu.SemaphoreType.DMA((copies,)),
                 pltpu.SemaphoreType.DMA((copies,)),
+                *(vmem(shape, F32) for shape in shapes),
             ],
             compiler_params=pltpu.CompilerParams(
                 collective_id=0, has_side_effects=True, vmem_limit_bytes=54_550_000

time: 49.4 us -> 47.4 us (0.960)
  Pallas kernels: 48.6 us -> 46.6 us
    pallas_call x1, Pallas kernels: 47.3 us -> 45.2 us  [shards(): pl.pallas_call(functools.partial(kernel, (nz, ny, nx), subjects), name='s...]
where the time goes in v3:
time: 47.4 us; the launch traced here: 47.2 us
  Pallas kernels  46.6 us (98%)
  between operations  0.64 us (1%)
    pallas_call x1, Pallas kernels, shards(): pl.pallas_call(functools.partial(kernel, (nz, ny, nx), subjects), name='s...  45.2 us
    pallas_call x1, Pallas kernels, shards(): pl.pallas_call(finish, name='srm_maps', out_shape=(jax.ShapeDtypeStruct((...  1.36 us

profile of v3, /device:TPU:1, one launch (start us, length us, event | category | flops | bytes accessed | tf_op | source)
XLA Modules:
  0.0 47.2 jit_solution(2486996925745267573)
XLA Ops:
  0.6 45.2 %srm_step.1 = (bf16[256,256]{1,0:T(8,128)(2,1)S(1)}, bf16[256,256]{1,0:T(8,128)(2,1)S(1)}, bf16[256,1024]{1,0:T(8,128)(2,1)S(1)}, bf16[256,1024]{1,0:T(8,128)(2,1)S(1)}, f32[450,256]{1,0:T(8,128)S(1)}) custom-call(bf16[1,450,1024]{2,1,0:T(8,128)(2,1)} %data_hbm.1, bf16[1,256,1024]{2,1,0:T(8,128)(2,1)} %maps_hbm.1), custom_call_target="tpu_custom_call" | custom-call | tf_op jit(solution)/shard_map/srm_step/pallas_call | solution.py:377
  45.9 1.4 %srm_maps.1 = (f32[450,256]{1,0:T(8,128)}, bf16[1,256,1024]{2,1,0:T(8,128)(2,1)}) custom-call(bf16[256,256]{1,0:T(8,128)(2,1)S(1)} %get-tuple-element.7.p_hi, bf16[256,256]{1,0:T(8,128)(2,1)S(1)} %get-tuple-element.8.p_lo, bf16[256,1024]{1,0:T(8,128)(2,1)S(1)} %get-tuple-element.9.a_hi, bf16[256,1024]{1,0:T(8,128)(2,1)S(1)} %get-tuple-element.10.a_lo, ...), custom_call_target="tpu_custom_call" | custom-call | tf_op jit(solution)/shard_map/srm_maps/pallas_call | solution.py:412

commit v4 on v3

--- a/solution.py
+++ b/solution.py
@@ -11,7 +11,7 @@
 NS_STEPS = 5
 LANES = 128
 ROWS = 512
-CHUNKS = 2
+CHUNKS = 4
 LAG = 4
 HALF = ROWS // 2
 C_X = 256
@@ -318,17 +318,30 @@
     unit = lax.broadcasted_iota(jnp.int32, (k, k), 0) == lax.broadcasted_iota(
         jnp.int32, (k, k), 1
     )
-    eye = jnp.where(unit, 1.5, 0.0).astype(F32)
-    middle = eye - 0.5 * estimate
-    both = jnp.concatenate([dot3(split(estimate), split(middle)), middle], axis=0)
-    a_hi[...], a_lo[...] = split(dot(shared_t, d[...]))
-    for step in range(1, NS_STEPS):
-        high, low_part = split(both)
-        inverse = (high[k:], low_part[k:])
-        middle = split(eye - 0.5 * dot3(inverse, (high[:k], low_part[:k])))
-        if step < NS_STEPS - 1:
-            both = dot3((high, low_part), middle)
-    p_hi[...], p_lo[...] = split(dot3(inverse, middle) * (1.0 / jnp.sqrt(scale)))
+    one = jnp.where(unit, 1.0, 0.0).astype(F32)
+    split_x = split(estimate)
+    product = None
+    for step_pair in range(NS_STEPS // 2):
+        x = estimate
+        xs = split_x
+        x2 = dot3(xs, xs)
+        quartic = dot3(split(x2), split(0.0625 * x2 - 0.5625 * x))
+        factor = split(2.25 * one - 2.4375 * x + 1.6875 * x2 + quartic)
+        if product is None:
+            a_hi[...], a_lo[...] = split(dot(shared_t, d[...]))
+            xq = dot3(xs, factor)
+            product = factor
+        else:
+            stacked = tuple(jnp.concatenate(pair, axis=0) for pair in zip(xs, product))
+            both = dot3(stacked, factor)
+            xq, product = both[:k], split(both[k:])
+        estimate = dot3(split(xq), factor)
+        split_x = split(estimate)
+    if NS_STEPS % 2:
+        inverse = dot3(split(1.5 * one - 0.5 * estimate), product)
+    else:
+        inverse = product[0].astype(F32) + product[1].astype(F32)
+    p_hi[...], p_lo[...] = split(inverse * (1.0 / jnp.sqrt(scale)))
     drain(len(pending))
 
 

time: 47.4 us -> 47 us (level)
  no operation moved by 1% of the time
where the time goes in v4:
time: 47 us; the launch traced here: 46.9 us
  Pallas kernels  46.2 us (98%)
  between operations  0.64 us (1%)
    pallas_call x1, Pallas kernels, shards(): pl.pallas_call(functools.partial(kernel, (nz, ny, nx), subjects), name='s...  44.9 us
    pallas_call x1, Pallas kernels, shards(): pl.pallas_call(finish, name='srm_maps', out_shape=(jax.ShapeDtypeStruct((...  1.36 us

profile of v4, /device:TPU:1, one launch (start us, length us, event | category | flops | bytes accessed | tf_op | source)
XLA Modules:
  0.0 46.9 jit_solution(17732419135249377215)
XLA Ops:
  0.6 44.9 %srm_step.1 = (bf16[256,256]{1,0:T(8,128)(2,1)S(1)}, bf16[256,256]{1,0:T(8,128)(2,1)S(1)}, bf16[256,1024]{1,0:T(8,128)(2,1)S(1)}, bf16[256,1024]{1,0:T(8,128)(2,1)S(1)}, f32[450,256]{1,0:T(8,128)S(1)}) custom-call(bf16[1,450,1024]{2,1,0:T(8,128)(2,1)} %data_hbm.1, bf16[1,256,1024]{2,1,0:T(8,128)(2,1)} %maps_hbm.1), custom_call_target="tpu_custom_call" | custom-call | tf_op jit(solution)/shard_map/srm_step/pallas_call | solution.py:390
  45.5 1.4 %srm_maps.1 = (f32[450,256]{1,0:T(8,128)}, bf16[1,256,1024]{2,1,0:T(8,128)(2,1)}) custom-call(bf16[256,256]{1,0:T(8,128)(2,1)S(1)} %get-tuple-element.7.p_hi, bf16[256,256]{1,0:T(8,128)(2,1)S(1)} %get-tuple-element.8.p_lo, bf16[256,1024]{1,0:T(8,128)(2,1)S(1)} %get-tuple-element.9.a_hi, bf16[256,1024]{1,0:T(8,128)(2,1)S(1)} %get-tuple-element.10.a_lo, ...), custom_call_target="tpu_custom_call" | custom-call | tf_op jit(solution)/shard_map/srm_maps/pallas_call | solution.py:425

commit v5 on v4

--- a/solution.py
+++ b/solution.py
@@ -14,12 +14,9 @@
 CHUNKS = 4
 LAG = 4
 HALF = ROWS // 2
-C_X = 256
 SUMS = (
     ("r", 0, HALF, "subj", ("x", "y")),
     ("r", HALF, HALF, "y", ("x", "subj")),
-    ("c", 0, C_X, "x", ("y",)),
-    ("c", C_X, ROWS - C_X, "y", ("x",)),
 )
 MESH = pl.DeviceIdType.MESH
 F32, BF16 = jnp.float32, jnp.bfloat16
@@ -236,6 +233,54 @@
         got_other[name].append(send(mine, mine, "core", 1, full.at[other, here]))
         yield
 
+    block_x = ROWS // nx
+    fine = block_x // ny
+
+    def gram_sum(buffers):
+        c1, c2_sum, c2 = buffers
+        got = {}
+
+        def place(x):
+            return rows(x * block_x, block_x)
+
+        def fine_place(x, y):
+            return rows(x * block_x + y * fine, fine)
+
+        for s in far_first(nx):
+            slot = c1.at[s - 1]
+            got[s] = send(sum_c.at[place(ahead("x", s))], slot, "x", s, slot)
+        yield
+        total = sum_c[place(me["x"])]
+        for s in near_first(nx):
+            got[s]()
+            total = total + c1[s - 1]
+        c2_sum[...] = total
+        for s in far_first(ny):
+            slot = c2.at[s - 1]
+            got[s] = send(c2_sum.at[rows(ahead("y", s) * fine, fine)], slot, "y", s, slot)
+        yield
+        total = c2_sum[rows(me["y"] * fine, fine)]
+        for s in far_first(ny):
+            got[s]()
+            total = total + c2[s - 1]
+        mine = full_c.at[core, fine_place(me["x"], me["y"])]
+        mine[...] = total
+        for s in far_first(ny):
+            there = full_c.at[core, fine_place(me["x"], behind("y", s))]
+            got[s] = send(mine, mine, "y", s, there)
+        yield
+        for s in far_first(ny):
+            got[s]()
+        mine = full_c.at[core, place(me["x"])]
+        for s in far_first(nx):
+            got[s] = send(mine, mine, "x", s, full_c.at[core, place(behind("x", s))])
+        yield
+        for s in near_first(nx):
+            got[s]()
+        mine = full_c.at[core]
+        got_other["c"].append(send(mine, mine, "core", 1, full_c.at[other]))
+        yield
+
     marks = []
     drained = 0
 
@@ -260,22 +305,22 @@
         )
         own = [next(rest) for _ in range(1 + len(others))]
         chains.append(summed(name, source, full, factor, start, count, axis, others, own))
-    r0, r1, c0, c1 = chains
+    r0, r1 = chains
+    c0 = gram_sum(list(rest))
     got_pair_r()
     sum_r[...] = part_r[core] + pair_r[...]
     step(r0, r1)
     got_pair_c()
     sum_c[...] = part_c[core] + pair_c[...]
-    step(c0, c1)
+    step(c0)
     step(c0)
     step(r0, r1)
-    step(c1)
     step(r0, r1)
-    step(c1)
     step(c0)
     step(r0, r1)
-    step(c0, c1)
+    step(c0)
     step(r0, r1)
+    step(c0)
     for wait in got_other["c"]:
         wait()
 
@@ -379,6 +424,9 @@
         shapes.append((size[axis] - 1, block, LANES))
         shapes += [(size[across], block, LANES) for across in others]
         copies += 2 * size[axis] - 1 + sum(size[across] - 1 for across in others)
+    block_x = ROWS // nx
+    shapes += [(nx - 1, block_x, LANES), (block_x, LANES), (ny - 1, block_x // ny, LANES)]
+    copies += 2 * (nx + ny)
 
     def shards(data, maps):
         _, trs, vectors = data.shape

time: 47 us -> 46.7 us (level)
  no operation moved by 1% of the time
where the time goes in v5:
time: 46.7 us; the launch traced here: 46.6 us
  Pallas kernels  45.9 us (98%)
  between operations  0.64 us (1%)
    pallas_call x1, Pallas kernels, shards(): pl.pallas_call(functools.partial(kernel, (nz, ny, nx), subjects), name='s...  44.6 us
    pallas_call x1, Pallas kernels, shards(): pl.pallas_call(finish, name='srm_maps', out_shape=(jax.ShapeDtypeStruct((...  1.36 us

profile of v5, /device:TPU:1, one launch (start us, length us, event | category | flops | bytes accessed | tf_op | source)
XLA Modules:
  0.0 46.6 jit_solution(148627670371682952)
XLA Ops:
  0.6 44.6 %srm_step.1 = (bf16[256,256]{1,0:T(8,128)(2,1)S(1)}, bf16[256,256]{1,0:T(8,128)(2,1)S(1)}, bf16[256,1024]{1,0:T(8,128)(2,1)S(1)}, bf16[256,1024]{1,0:T(8,128)(2,1)S(1)}, f32[450,256]{1,0:T(8,128)S(1)}) custom-call(bf16[1,450,1024]{2,1,0:T(8,128)(2,1)} %data_hbm.1, bf16[1,256,1024]{2,1,0:T(8,128)(2,1)} %maps_hbm.1), custom_call_target="tpu_custom_call" | custom-call | tf_op jit(solution)/shard_map/srm_step/pallas_call | solution.py:438
  45.2 1.4 %srm_maps.1 = (f32[450,256]{1,0:T(8,128)}, bf16[1,256,1024]{2,1,0:T(8,128)(2,1)}) custom-call(bf16[256,256]{1,0:T(8,128)(2,1)S(1)} %get-tuple-element.7.p_hi, bf16[256,256]{1,0:T(8,128)(2,1)S(1)} %get-tuple-element.8.p_lo, bf16[256,1024]{1,0:T(8,128)(2,1)S(1)} %get-tuple-element.9.a_hi, bf16[256,1024]{1,0:T(8,128)(2,1)S(1)} %get-tuple-element.10.a_lo, ...), custom_call_target="tpu_custom_call" | custom-call | tf_op jit(solution)/shard_map/srm_maps/pallas_call | solution.py:473

commit v6 on v5

--- a/solution.py
+++ b/solution.py
@@ -96,16 +96,17 @@
         loads.append((part, load_d, load_w))
 
     barrier = pltpu.get_barrier_semaphore()
-    partners = 0
-    for axis, n in size.items():
-        for s in range(1, n):
-            pl.semaphore_signal(
-                barrier,
-                inc=1,
-                device_id={axis: lax.rem(me[axis] + s, n)},
-                device_id_type=MESH,
-            )
-            partners += 1
+    partners = sorted(
+        ((axis, s) for axis, n in size.items() for s in range(1, n)),
+        key=lambda p: -min(p[1], size[p[0]] - p[1]),
+    )
+    for axis, s in partners:
+        pl.semaphore_signal(
+            barrier,
+            inc=1,
+            device_id={axis: lax.rem(me[axis] + s, size[axis])},
+            device_id_type=MESH,
+        )
 
     pending = []
 
@@ -164,7 +165,7 @@
         partial = term if partial is None else partial + term
     part_r[0] = partial[:, :LANES]
     part_r[1] = partial[:, LANES:]
-    pl.semaphore_wait(barrier, partners)
+    pl.semaphore_wait(barrier, len(partners))
     got_pair_r = send(part_r.at[other], pair_r, "core", 1, pair_r)
 
     row = lax.broadcasted_iota(jnp.int32, (LANES, LANES), 0)

time: 46.7 us -> 46.1 us (0.987)
  Pallas kernels: 45.9 us -> 45.3 us
    pallas_call x1, Pallas kernels: 44.6 us -> 44 us  [shards(): pl.pallas_call(functools.partial(kernel, (nz, ny, nx), subjects), name='s...]
where the time goes in v6:
time: 46.1 us; the launch traced here: 46 us
  Pallas kernels  45.3 us (98%)
  between operations  0.64 us (1%)
    pallas_call x1, Pallas kernels, shards(): pl.pallas_call(functools.partial(kernel, (nz, ny, nx), subjects), name='s...  44 us
    pallas_call x1, Pallas kernels, shards(): pl.pallas_call(finish, name='srm_maps', out_shape=(jax.ShapeDtypeStruct((...  1.36 us

profile of v6, /device:TPU:1, one launch (start us, length us, event | category | flops | bytes accessed | tf_op | source)
XLA Modules:
  0.0 46.0 jit_solution(4175005728227226789)
XLA Ops:
  0.6 44.0 %srm_step.1 = (bf16[256,256]{1,0:T(8,128)(2,1)S(1)}, bf16[256,256]{1,0:T(8,128)(2,1)S(1)}, bf16[256,1024]{1,0:T(8,128)(2,1)S(1)}, bf16[256,1024]{1,0:T(8,128)(2,1)S(1)}, f32[450,256]{1,0:T(8,128)S(1)}) custom-call(bf16[1,450,1024]{2,1,0:T(8,128)(2,1)} %data_hbm.1, bf16[1,256,1024]{2,1,0:T(8,128)(2,1)} %maps_hbm.1), custom_call_target="tpu_custom_call" | custom-call | tf_op jit(solution)/shard_map/srm_step/pallas_call | solution.py:439
  44.6 1.4 %srm_maps.1 = (f32[450,256]{1,0:T(8,128)}, bf16[1,256,1024]{2,1,0:T(8,128)(2,1)}) custom-call(bf16[256,256]{1,0:T(8,128)(2,1)S(1)} %get-tuple-element.7.p_hi, bf16[256,256]{1,0:T(8,128)(2,1)S(1)} %get-tuple-element.8.p_lo, bf16[256,1024]{1,0:T(8,128)(2,1)S(1)} %get-tuple-element.9.a_hi, bf16[256,1024]{1,0:T(8,128)(2,1)S(1)} %get-tuple-element.10.a_lo, ...), custom_call_target="tpu_custom_call" | custom-call | tf_op jit(solution)/shard_map/srm_maps/pallas_call | solution.py:474

commit v7 on v6

--- a/solution.py
+++ b/solution.py
@@ -205,7 +205,7 @@
         for s in far_first(n):
             slot = arrived.at[s - 1]
             got[s] = send(source.at[place(ahead(axis, s))], slot, axis, s, slot)
-        yield
+            yield
         total = source[place(me[axis])]
         for s in far_first(n):
             got[s]()
@@ -310,6 +310,9 @@
     c0 = gram_sum(list(rest))
     got_pair_r()
     sum_r[...] = part_r[core] + pair_r[...]
+    for _ in range(nz - 2):
+        next(r0)
+        next(r1)
     step(r0, r1)
     got_pair_c()
     sum_c[...] = part_c[core] + pair_c[...]

time: 46.1 us -> 46.1 us (level)
  no operation moved by 1% of the time
where the time goes in v7:
time: 46.1 us; the launch traced here: 46 us
  Pallas kernels  45.3 us (98%)
  between operations  0.64 us (1%)
    pallas_call x1, Pallas kernels, shards(): pl.pallas_call(functools.partial(kernel, (nz, ny, nx), subjects), name='s...  44 us
    pallas_call x1, Pallas kernels, shards(): pl.pallas_call(finish, name='srm_maps', out_shape=(jax.ShapeDtypeStruct((...  1.36 us

profile of v7, /device:TPU:1, one launch (start us, length us, event | category | flops | bytes accessed | tf_op | source)
XLA Modules:
  0.0 46.0 jit_solution(16973284382562234679)
XLA Ops:
  0.6 44.0 %srm_step.1 = (bf16[256,256]{1,0:T(8,128)(2,1)S(1)}, bf16[256,256]{1,0:T(8,128)(2,1)S(1)}, bf16[256,1024]{1,0:T(8,128)(2,1)S(1)}, bf16[256,1024]{1,0:T(8,128)(2,1)S(1)}, f32[450,256]{1,0:T(8,128)S(1)}) custom-call(bf16[1,450,1024]{2,1,0:T(8,128)(2,1)} %data_hbm.1, bf16[1,256,1024]{2,1,0:T(8,128)(2,1)} %maps_hbm.1), custom_call_target="tpu_custom_call" | custom-call | tf_op jit(solution)/shard_map/srm_step/pallas_call | solution.py:442
  44.6 1.4 %srm_maps.1 = (f32[450,256]{1,0:T(8,128)}, bf16[1,256,1024]{2,1,0:T(8,128)(2,1)}) custom-call(bf16[256,256]{1,0:T(8,128)(2,1)S(1)} %get-tuple-element.7.p_hi, bf16[256,256]{1,0:T(8,128)(2,1)S(1)} %get-tuple-element.8.p_lo, bf16[256,1024]{1,0:T(8,128)(2,1)S(1)} %get-tuple-element.9.a_hi, bf16[256,1024]{1,0:T(8,128)(2,1)S(1)} %get-tuple-element.10.a_lo, ...), custom_call_target="tpu_custom_call" | custom-call | tf_op jit(solution)/shard_map/srm_maps/pallas_call | solution.py:477
